TPU v7x, 32 devices: a whole 2x2x4 slice. The times are simulated.
32 devices in a mesh: dp: 16 (over z, y, core), tensor: 2 (over x).
Axes of the slice: x: 2, y: 2, z: 4, core: 2. Of those that a mesh axis runs over, the one named last changes fastest.
Arguments:
- normed_input: bfloat16 [2048, 8192], P('dp', 'tensor'), may hold values from -6 to 6
- key_cotangent: bfloat16 [2048, 1024], P('dp', 'tensor'), may hold values from -6 to 6
- frozen_key_weight: bfloat16 [8192, 1024], P(None, 'tensor'), may hold values from -0.1875 to 0.1875
- adapter_down_maps: bfloat16 [32, 8192, 16], P(None, 'tensor'), may hold values from -0.0625 to 0.0625
- adapter_up_maps: bfloat16 [32, 16, 1024], P(None, None, 'tensor'), may hold values from -0.1875 to 0.1875
- document_of_token: int32 [2048], P('dp'), may hold values from 0 to 31, never falling along the last dimension, each value on 1 to 512 neighbouring positions
- tenant_of_document: int32 [32], replicated, may hold values from 0 to 31
- tenant_slot_index: int32 [32], replicated, may hold values from 0 to 31, each once
Outputs:
- input_gradient: bfloat16 [2048, 8192], P('dp', 'tensor')
- down_gradient: bfloat16 [32, 8192, 16], P(None, 'tensor')
- up_gradient: bfloat16 [32, 16, 1024], P(None, None, 'tensor')
Inputs may be any that keep to these rules, and one draw needn't show every extreme that they name: `document_of_token`: never falling along the tokens; each document 1 to (512) tokens. `tenant_slot_index`: each slot once.
All inputs are finite; a program needn't handle non-finite values.
Results may differ from a plain program's by a relative error of at most 0.008.
Values may be sent and summed in bfloat16 or wider, within the bound.
A program may use at most 64 MiB of HBM per device.

v0:
```python
import jax
import jax.numpy as jnp
from jax import lax
from jax.sharding import PartitionSpec as P

adapter_scale = 2.0


def per_device(
    normed_input,
    key_cotangent,
    frozen_key_weight,
    adapter_down_maps,
    adapter_up_maps,
    document_of_token,
    tenant_of_document,
    tenant_slot_index,
):
    tenant_count, token_rows, adapter_rank = adapter_down_maps.shape
    key_heads_width = adapter_up_maps.shape[2]
    slot = jnp.take(tenant_slot_index, jnp.take(tenant_of_document, document_of_token))
    member = (slot[:, None] == jnp.arange(tenant_count, dtype=jnp.int32)[None, :]).astype(
        jnp.float32
    )
    down_flattened = jnp.transpose(adapter_down_maps, (1, 0, 2)).reshape(
        token_rows, tenant_count * adapter_rank
    )
    up_flattened = jnp.transpose(adapter_up_maps, (2, 0, 1)).reshape(
        key_heads_width, tenant_count * adapter_rank
    )
    h_all = jnp.dot(normed_input, down_flattened, preferred_element_type=jnp.float32).reshape(
        -1, tenant_count, adapter_rank
    )
    g_all = jnp.dot(key_cotangent, up_flattened, preferred_element_type=jnp.float32).reshape(
        -1, tenant_count, adapter_rank
    )
    h_part = jnp.sum(h_all * member[:, :, None], axis=1)
    g_part = jnp.sum(g_all * member[:, :, None], axis=1)
    h_total, g_total = lax.psum((h_part, g_part), "tensor")
    low_h = h_total.astype(jnp.bfloat16)
    low_g = g_total.astype(jnp.bfloat16)
    spread_hidden = (
        (member[:, :, None] * low_h.astype(jnp.float32)[:, None, :])
        .astype(jnp.bfloat16)
        .reshape(-1, tenant_count * adapter_rank)
    )
    spread_cotangent = (
        (member[:, :, None] * low_g.astype(jnp.float32)[:, None, :])
        .astype(jnp.bfloat16)
        .reshape(-1, tenant_count * adapter_rank)
    )
    down_gradient_piece = adapter_scale * jnp.dot(
        normed_input.T, spread_cotangent, preferred_element_type=jnp.float32
    )
    up_gradient_piece = adapter_scale * jnp.dot(
        spread_hidden.T, key_cotangent, preferred_element_type=jnp.float32
    )
    grad_a_sum, grad_b_sum = lax.psum((down_gradient_piece, up_gradient_piece), "dp")
    frozen_output = lax.psum_scatter(
        jnp.dot(frozen_key_weight, key_cotangent.T, preferred_element_type=jnp.float32),
        "tensor",
        scatter_dimension=0,
        tiled=True,
    ).T
    adapter_output = jnp.dot(spread_cotangent, down_flattened.T, preferred_element_type=jnp.float32)
    input_gradient = (frozen_output + adapter_scale * adapter_output).astype(jnp.bfloat16)
    down_gradient = jnp.transpose(
        grad_a_sum.reshape(token_rows, tenant_count, adapter_rank), (1, 0, 2)
    ).astype(jnp.bfloat16)
    up_gradient = grad_b_sum.reshape(tenant_count, adapter_rank, key_heads_width).astype(
        jnp.bfloat16
    )
    return (input_gradient, down_gradient, up_gradient)


def solution(mesh):
    in_specs = (
        P("dp", "tensor"),
        P("dp", "tensor"),
        P(None, "tensor"),
        P(None, "tensor", None),
        P(None, None, "tensor"),
        P("dp"),
        P(),
        P(),
    )
    out_specs = (P("dp", "tensor"), P(None, "tensor", None), P(None, None, "tensor"))
    return jax.shard_map(
        per_device, mesh=mesh, in_specs=in_specs, out_specs=out_specs, check_vma=False
    )
```

profile of v0, /device:TPU:1, one launch (start us, length us, event | category | flops | bytes accessed | tf_op | source)
XLA Modules:
  0.0 258.8 jit_solution(4367594680355027859)
XLA Ops:
  7.2 0.0 copy-start
  7.2 0.0 reduce-scatter.2.cloned.1.call-start
  7.2 7.8 %fusion.17 = f32[8192,128]{1,0:T(8,128)} fusion(bf16[8192,512]{1,0:T(8,128)(2,1)} %param.12, bf16[128,512]{1,0:T(8,128)(2,1)} %param.11), kind=kOutput, calls=%fused_computation.30 | convolution fusion | flops 1073741824 | bytes 12713984 | tf_op jit(solution)/shard_map/dot_general | solution.py:60
  15.0 0.0 copy-start.5
  15.0 0.0 copy-start.4
  15.0 0.0 reduce-scatter.2.cloned.1.call-update
  15.1 0.6 copy-done.5
  15.7 0.0 copy-done.1
  15.7 1.2 gather_fusion
  16.9 0.0 copy-done.2
  17.0 1.2 gather_fusion.1
  18.2 0.0 copy-done.3
  18.2 0.0 copy-done.4
  18.2 0.5 fusion.9
  18.7 0.0 copy-done
  18.7 5.1 %fusion.10 = f32[128,16]{0,1:T(8,128)S(1)} fusion(bf16[32,16,4096]{2,1,0:T(8,128)(2,1)} %bitcast.44, bf16[128,4096]{1,0:T(8,128)(2,1)S(1)} %copy-done, f32[128,32]{0,1:T(8,128)S(1)} %fusion.16), kind=kOutput, calls=%fused_computation.14 | convolution fusion | flops 536999936 | bytes 5267456 | tf_op jit(solution)/shard_map/dot_general | solution.py:31
  23.9 8.3 %all-reduce.1 = (bf16[128,16]{0,1:T(8,128)(2,1)S(1)}, bf16[128,16]{0,1:T(8,128)(2,1)S(1)}) all-reduce(f32[128,16]{0,1:T(8,128)S(1)} %fusion.9, f32[128,16]{0,1:T(8,128)S(1)} %fusion.10), channel_id=1, replica_groups=mesh['dp'=16,'tensor'=2] {'tensor'}, use_global_device_ids=true, to_apply=%region_2.4 | all-reduce | flops 4096 | bytes 24576 | tf_op jit(solution)/shard_map/psum | solution.py:39
  32.2 0.1 copy.17
  32.3 4.5 %multiply_bitcast_fusion = f32[4096,512]{0,1:T(8,128)} fusion(bf16[128,512]{0,1:T(8,128)(2,1)S(1)} %bitcast.46, bf16[128,4096]{1,0:T(8,128)(2,1)S(1)} %copy-done), kind=kOutput, calls=%fused_computation.2 | convolution fusion | flops 538968064 | bytes 9568256 | tf_op jit(solution)/shard_map/dot_general | solution.py:52
  36.7 0.1 copy.19
  36.8 0.3 convolution_multiply_fusion
  37.1 207.7 %all-reduce.3 = (bf16[4096,512]{0,1:T(8,128)(2,1)}, bf16[512,512]{1,0:T(8,128)(2,1)}) all-reduce(f32[4096,512]{0,1:T(8,128)} %multiply_bitcast_fusion, f32[512,512]{1,0:T(8,128)S(1)} %convolution_multiply_fusion), channel_id=1, replica_groups=mesh['dp'=16,'tensor'=2] {'dp'}, use_global_device_ids=true, to_apply=%region_3.5 | all-reduce | flops 2359296 | bytes 14155776 | tf_op jit(solution)/shard_map/psum | solution.py:58
  244.8 5.9 %fusion.2 = bf16[128,4096]{0,1:T(8,128)(2,1)S(1)} fusion(bf16[4096,32,16]{0,2,1:T(8,128)(2,1)} %bitcast.45, f32[4096,128]{1,0:T(8,128)} %reduce-scatter.2.cloned.1.call-done, f32[128,16]{0,1:T(8,128)S(1)} %convert_element_type.76, f32[128,32]{0,1:T(8,128)S(1)} %fusion.16), kind=kOutput, calls=%fused_computation.6 | convolution fusion | flops 538574848 | bytes 7364608 | tf_op jit(solution)/shard_map/dot_general | solution.py:65
  250.7 1.3 copy.20
  (13 shorter events, 0.1 us)
Async XLA Ops:
  7.2 11.5 %copy-start = (bf16[128,4096]{1,0:T(8,128)(2,1)S(1)}, bf16[128,4096]{1,0:T(8,128)(2,1)}, u32[]{:S(2)}) copy-start(bf16[128,4096]{1,0:T(8,128)(2,1)} %param.10) | copy-start | bytes 3145732
  7.2 237.6 %reduce-scatter.2.cloned.1.call-start = ((), (), s32[]{:S(2)}) async-start(), calls=%async_computation.1 | async-start | bytes 6291456 | tf_op jit(solution)/shard_map/reduce_scatter | solution.py:59
  15.0 0.7 copy-start.5
  15.0 0.7 copy-start.1
  15.0 1.9 copy-start.2
  15.0 3.2 %copy-start.3 = (bf16[128,512]{1,0:T(8,128)(2,1)S(1)}, bf16[128,512]{1,0:T(8,128)(2,1)}, u32[]{:S(2)}) copy-start(bf16[128,512]{1,0:T(8,128)(2,1)} %param.11) | copy-start | bytes 393220
  15.0 3.2 %copy-start.4 = (bf16[32,16,512]{2,1,0:T(8,128)(2,1)S(1)}, bf16[32,16,512]{2,1,0:T(8,128)(2,1)}, u32[]{:S(2)}) copy-start(bf16[32,16,512]{2,1,0:T(8,128)(2,1)} %param.14) | copy-start | bytes 1572868
Sparse Core Ops, SparseCore 0:
  15.2 56.6 reduce-scatter.1
where the time goes:
time: 259 us
  blocking collectives  216 us (83%)
  matrix products  24 us (9%)
  between operations  14.2 us (5%)
  local copies, waits for them, and re-layouts  4.51 us (2%)
    psum x1, blocking collectives, per_device(): lax.psum((down_gradient_piece, up_gradient_piece), 'dp')  208 us
    psum x1, blocking collectives, per_device(): h_total, g_total = lax.psum((h_part, g_part), 'tensor')  8.29 us
    dot_general x1, matrix products, per_device(): jnp.dot(frozen_key_weight, key_cotangent.T, preferred_element_type=jnp.fl...  7.78 us
    dot_general x1, matrix products, per_device(): jnp.dot(spread_cotangent, down_flattened.T, preferred_element_type=jnp.fl...  5.91 us
  transfers between devices with their start and end apart: 1, of which 0 were waited for; matrix products, arithmetic and copies ran while one was open for 5% of the time, Pallas kernels for 0%

commit v1 on v0

v1 whole, which is shorter than its diff:
```python
import jax
import jax.numpy as jnp
from jax import lax
from jax.sharding import PartitionSpec as P

adapter_scale = 2.0


def per_device(
    dp_count,
    tensor_count,
    normed_input,
    key_cotangent,
    frozen_key_weight,
    adapter_down_maps,
    adapter_up_maps,
    document_of_token,
    tenant_of_document,
    tenant_slot_index,
):
    tenant_count, token_rows, adapter_rank = adapter_down_maps.shape
    key_heads_width = adapter_up_maps.shape[2]
    tokens = normed_input.shape[0]
    doc_count = tenant_of_document.shape[0]
    pairs = tenant_count * adapter_rank
    bf16, f32 = jnp.bfloat16, jnp.float32
    tenants = jnp.arange(tenant_count, dtype=jnp.int32)
    slot_of_doc = jnp.sum(
        jnp.where(tenant_of_document[:, None] == tenants[None, :], tenant_slot_index[None, :], 0), axis=1
    )
    docs = jnp.arange(doc_count, dtype=jnp.int32)
    slot = jnp.sum(
        jnp.where(document_of_token[:, None] == docs[None, :], slot_of_doc[None, :], 0), axis=1
    )
    member = (slot[:, None] == tenants[None, :]).astype(f32)
    down_rows = jnp.transpose(adapter_down_maps, (0, 2, 1)).reshape(pairs, token_rows)
    up_rows = adapter_up_maps.reshape(pairs, key_heads_width)
    contract_last = (((1,), (1,)), ((), ()))
    h_all = lax.dot_general(normed_input, down_rows, contract_last, preferred_element_type=f32)
    g_all = lax.dot_general(key_cotangent, up_rows, contract_last, preferred_element_type=f32)
    h_part = jnp.sum(h_all.reshape(-1, tenant_count, adapter_rank) * member[:, :, None], axis=1)
    g_part = jnp.sum(g_all.reshape(-1, tenant_count, adapter_rank) * member[:, :, None], axis=1)
    low = lax.psum(jnp.concatenate([h_part, g_part], axis=1), "tensor").astype(bf16)

    x_all = lax.all_to_all(
        normed_input.reshape(tokens, dp_count, -1), "dp", split_axis=1, concat_axis=0, tiled=True
    ).reshape(tokens * dp_count, -1)
    k_all = lax.all_to_all(
        key_cotangent.reshape(tokens, dp_count, -1), "dp", split_axis=1, concat_axis=0, tiled=True
    ).reshape(tokens * dp_count, -1)
    tagged = jnp.concatenate([low, slot[:, None].astype(bf16)], axis=1)
    tagged_all = lax.all_gather(tagged, "dp", axis=0, tiled=True)
    slot_all = tagged_all[:, 2 * adapter_rank].astype(jnp.int32)
    member_all = (slot_all[:, None] == tenants[None, :]).astype(bf16)

    def spread(m, v):
        return (m[:, :, None] * v[:, None, :]).reshape(-1, pairs)

    spread_h = spread(member_all, tagged_all[:, :adapter_rank])
    spread_g_all = spread(member_all, tagged_all[:, adapter_rank : 2 * adapter_rank])
    contract_first = (((0,), (0,)), ((), ()))
    down_piece = (
        adapter_scale * lax.dot_general(spread_g_all, x_all, contract_first, preferred_element_type=f32)
    ).astype(bf16)
    up_piece = (
        adapter_scale * lax.dot_general(spread_h, k_all, contract_first, preferred_element_type=f32)
    ).astype(bf16)
    down_flat = lax.all_gather(down_piece, "dp", axis=1, tiled=True)
    up_flat = lax.all_gather(up_piece, "dp", axis=1, tiled=True)

    frozen = lax.dot_general(
        key_cotangent, frozen_key_weight, contract_last, preferred_element_type=f32
    )
    frozen_output = lax.psum_scatter(frozen.astype(bf16), "tensor", scatter_dimension=1, tiled=True)
    spread_g = spread(member.astype(bf16), low[:, adapter_rank:])
    adapter_output = jnp.dot(spread_g, down_rows, preferred_element_type=f32)
    input_gradient = (frozen_output.astype(f32) + adapter_scale * adapter_output).astype(bf16)
    down_gradient = jnp.transpose(
        down_flat.reshape(tenant_count, adapter_rank, token_rows), (0, 2, 1)
    )
    up_gradient = up_flat.reshape(tenant_count, adapter_rank, key_heads_width)
    return (input_gradient, down_gradient, up_gradient)


def solution(mesh):
    in_specs = (
        P("dp", "tensor"),
        P("dp", "tensor"),
        P(None, "tensor"),
        P(None, "tensor", None),
        P(None, None, "tensor"),
        P("dp"),
        P(),
        P(),
    )
    out_specs = (P("dp", "tensor"), P(None, "tensor", None), P(None, None, "tensor"))

    def body(*args):
        return per_device(mesh.shape["dp"], mesh.shape["tensor"], *args)

    return jax.shard_map(body, mesh=mesh, in_specs=in_specs, out_specs=out_specs, check_vma=False)
```

time: 259 us -> 134 us (0.52)
  blocking collectives: 216 us -> 54.6 us
  waiting for transfers between devices: 0.02 us -> 15.9 us
  starting transfers between devices: 0.04 us -> 10.9 us
  local copies, waits for them, and re-layouts: 4.51 us -> 11.3 us
    psum x2 -> x1, blocking collectives: 216 us -> 7.53 us  [per_device(): lax.psum(jnp.concatenate([h_part, g_part], axis=1), 'tensor').astype(bf16)]
    all_gather x0 -> x2, blocking collectives: none -> 47 us  [the longest x1 23.6 us: per_device(): up_flat = lax.all_gather(up_piece, 'dp', axis=1, tiled=True)]
    all_to_all x0 -> x2, starting transfers between devices: none -> 10.8 us  [the longest x1 7.34 us: per_device(): lax.all_to_all(normed_input.reshape(tokens, dp_count, -1), 'dp', split_ax...]
    all_gather x0 -> x1, waiting for transfers between devices: none -> 8.96 us  [per_device(): down_flat = lax.all_gather(down_piece, 'dp', axis=1, tiled=True)]
    all_to_all x0 -> x2, waiting for transfers between devices: none -> 6.89 us  [the longest x1 6.89 us: per_device(): lax.all_to_all(key_cotangent.reshape(tokens, dp_count, -1), 'dp', split_a...]
    unnamed x13 -> x17, local copies, waits for them, and re-layouts: 1.95 us -> 7.99 us
  transfers between devices with their start and end apart: 1 -> 4, of which waited for: 0 -> 2; matrix products, arithmetic and copies ran while one was open for 5% -> 17% of each run, Pallas kernels for 0% -> 0%
where the time goes in v1:
time: 134 us
  blocking collectives  54.6 us (41%)
  matrix products  23.4 us (17%)
  waiting for transfers between devices  15.9 us (12%)
  between operations  15.6 us (12%)
  local copies, waits for them, and re-layouts  11.3 us (8%)
  starting transfers between devices  10.9 us (8%)
  other arithmetic  1.93 us (1%)
    all_gather x1, blocking collectives, per_device(): up_flat = lax.all_gather(up_piece, 'dp', axis=1, tiled=True)  23.6 us
    all_gather x1, blocking collectives, per_device(): tagged_all = lax.all_gather(tagged, 'dp', axis=0, tiled=True)  23.4 us
    all_gather x1, waiting for transfers between devices, per_device(): down_flat = lax.all_gather(down_piece, 'dp', axis=1, tiled=True)  8.96 us
    unnamed x17, local copies, waits for them, and re-layouts  7.99 us
    dot_general x1, matrix products, per_device(): lax.dot_general(key_cotangent, frozen_key_weight, contract_last, preferre...  7.64 us
    psum x1, blocking collectives, per_device(): lax.psum(jnp.concatenate([h_part, g_part], axis=1), 'tensor').astype(bf16)  7.53 us
    all_to_all x1, starting transfers between devices, per_device(): lax.all_to_all(normed_input.reshape(tokens, dp_count, -1), 'dp', split_ax...  7.34 us
    all_to_all x1, waiting for transfers between devices, per_device(): lax.all_to_all(key_cotangent.reshape(tokens, dp_count, -1), 'dp', split_a...  6.89 us
  transfers between devices with their start and end apart: 4, of which 2 were waited for; matrix products, arithmetic and copies ran while one was open for 17% of the time, Pallas kernels for 0%

profile of v1, /device:TPU:1, one launch (start us, length us, event | category | flops | bytes accessed | tf_op | source)
XLA Modules:
  0.0 133.6 jit_solution(16899172120371347481)
XLA Ops:
  8.1 7.6 %convolution_convert_fusion = bf16[128,8192]{1,0:T(8,128)(2,1)} fusion(bf16[128,512]{1,0:T(8,128)(2,1)} %param.9, bf16[8192,512]{1,0:T(8,128)(2,1)} %param.10), kind=kOutput, calls=%fused_computation | convolution fusion | flops 1074790400 | bytes 10616832 | tf_op jit(solution)/shard_map/dot_general | solution.py:71
  15.7 1.2 copy-done.1
  16.9 1.3 copy.34
  18.2 7.3 %all-to-all-start = ((bf16[128,16,256]{0,2,1:T(8,128)(2,1)}), bf16[128,16,256]{0,2,1:T(8,128)(2,1)}, u32[]{:S(2)}, u32[]{:S(2)}) async-start(bf16[128,16,256]{0,2,1:T(8,128)(2,1)} %bitcast.7), calls=%async_computation.1 | async-start | bytes 2097152 | tf_op jit(solution)/shard_map/all_to_all | solution.py:45
  25.6 0.0 all-gather.2.cloned.1.call-start
  25.6 0.2 select_reduce_fusion.1
  25.8 0.1 select_reduce_fusion
  26.0 0.5 fusion.10
  26.4 5.1 %fusion.11 = f32[128,16]{0,1:T(8,128)S(1)} fusion(bf16[32,16,4096]{2,1,0:T(8,128)(2,1)} %bitcast.53, bf16[128,4096]{1,0:T(8,128)(2,1)S(1)} %copy-done.1, f32[128,32]{0,1:T(8,128)S(1)} %get-tuple-element.11), kind=kOutput, calls=%fused_computation.13 | convolution fusion | flops 536999936 | bytes 5267456 | tf_op jit(solution)/shard_map/dot_general | solution.py:39
  31.6 7.5 %psum.7 = bf16[128,32]{0,1:T(8,128)(2,1)S(1)} all-reduce(f32[128,32]{0,1:T(8,128)S(1)} %pad_maximum_fusion), channel_id=1, replica_groups=mesh['dp'=16,'tensor'=2] {'tensor'}, use_global_device_ids=true, to_apply=%region_5.6 | all-reduce | flops 4096 | bytes 24576 | tf_op jit(solution)/shard_map/psum | solution.py:43
  39.1 23.4 %all_gather.9 = bf16[2048,33]{0,1:T(8,128)(2,1)S(1)} all-gather(bf16[128,33]{0,1:T(8,128)(2,1)S(1)} %pad_maximum_fusion.1), channel_id=1, replica_groups=mesh['dp'=16,'tensor'=2] {'dp'}, dimensions={0}, use_global_device_ids=true | all-gather | bytes 143616 | tf_op jit(solution)/shard_map/all_gather | solution.py:52
  62.6 1.6 %broadcast_multiply_fusion = (bf16[2048,32,16]{0,2,1:T(8,128)(2,1)S(1)}, bf16[2048,32,16]{0,2,1:T(8,128)(2,1)}) fusion(bf16[2048,16]{0,1:T(8,128)(2,1)S(1)} %get-tuple-element.6, bf16[2048,32]{0,1:T(8,128)(2,1)S(1)} %fusion.17, bf16[2048,16]{0,1:T(8,128)(2,1)S(1)} %get-tuple-element.7), kind=kLoop, calls=%fused_computation.17 | loop fusion | flops 2097152 | bytes 4456448 | tf_op jit(solution)/shard_map/mul | solution.py:57
  64.2 2.3 %copy.35 = bf16[16,128,1,256]{3,1,0,2:T(8,128)(2,1)} copy(bf16[16,128,1,256]{1,3,0,2:T(8,128)(2,1)} %bitcast.9) | data formatting | bytes 2097152 | tf_op jit(solution)/shard_map/all_to_all | solution.py:45
  66.5 3.3 %fusion.6 = bf16[512,256]{1,0:T(8,128)(2,1)} fusion(bf16[2048,512]{0,1:T(8,128)(2,1)} %bitcast.47, bf16[2048,256]{1,0:T(8,128)(2,1)} %bitcast.48), kind=kOutput, calls=%fused_computation.9 | convolution fusion | flops 537133056 | bytes 3407872 | tf_op jit(solution)/shard_map/dot_general | solution.py:63
  69.8 0.8 copy.36
  70.5 3.5 %all-to-all-start.1 = ((bf16[128,16,32]{0,2,1:T(8,128)(2,1)}), bf16[128,16,32]{0,2,1:T(8,128)(2,1)S(1)}, u32[]{:S(2)}, u32[]{:S(2)}) async-start(bf16[128,16,32]{0,2,1:T(8,128)(2,1)} %bitcast.14), calls=%async_computation.2 | async-start | bytes 262144 | tf_op jit(solution)/shard_map/all_to_all | solution.py:48
  74.0 6.9 %all-to-all-done.1 = bf16[128,16,32]{0,2,1:T(8,128)(2,1)S(1)} async-done(((bf16[128,16,32]{0,2,1:T(8,128)(2,1)}), bf16[128,16,32]{0,2,1:T(8,128)(2,1)S(1)}, u32[]{:S(2)}, u32[]{:S(2)}) %all-to-all-start.1) | async-done | bytes 131104 | tf_op jit(solution)/shard_map/all_to_all | solution.py:48
  80.9 0.1 copy.37
  80.9 0.7 fusion.14
  81.7 23.6 %all_gather.11 = bf16[512,512]{0,1:T(8,128)(2,1)S(1)} all-gather(bf16[512,32]{0,1:T(8,128)(2,1)S(1)} %fusion.14), channel_id=1, replica_groups=mesh['dp'=16,'tensor'=2] {'dp'}, dimensions={1}, use_global_device_ids=true | all-gather | bytes 557056 | tf_op jit(solution)/shard_map/all_gather | solution.py:69
  105.3 1.0 copy.38
  106.3 6.2 %fusion.2 = bf16[128,4096]{1,0:T(8,128)(2,1)} fusion(bf16[32,16,4096]{2,1,0:T(8,128)(2,1)} %bitcast.54, bf16[128,4096]{1,0:T(8,128)(2,1)} %reduce-scatter.2.cloned.1.call-done, bf16[128,16]{0,1:T(8,128)(2,1)S(1)} %slice-done, bf16[128,32]{0,1:T(8,128)(2,1)S(1)} %get-tuple-element.10), kind=kOutput, calls=%fused_computation.4 | convolution fusion | flops 539033600 | bytes 6303744 | tf_op jit(solution)/shard_map/dot_general | solution.py:76
  112.5 9.0 %all-gather.2.cloned.1.call-done = bf16[512,4096]{1,0:T(8,128)(2,1)} async-done(((bf16[512,256]{1,0:T(8,128)(2,1)}), bf16[512,4096]{1,0:T(8,128)(2,1)}) %all-gather.2.cloned.1.call-update) | async-done | bytes 4194320 | tf_op jit(solution)/shard_map/all_gather | solution.py:68
  121.4 4.7 %copy.55 = bf16[32,4096,16]{1,2,0:T(8,128)(2,1)} copy(bf16[32,4096,16]{1,2,0:T(8,128)(2,1)} %bitcast.46) | data formatting | bytes 8388608
  (27 shorter events, 0.2 us)
Async XLA Ops:
  8.0 17.9 %copy-start = (bf16[32,16,512]{2,1,0:T(8,128)(2,1)S(1)}, bf16[32,16,512]{2,1,0:T(8,128)(2,1)}, u32[]{:S(2)}) copy-start(bf16[32,16,512]{2,1,0:T(8,128)(2,1)} %param.12) | copy-start | bytes 1572868
  8.0 98.3 %reduce-scatter.2.cloned.1.call-start = ((), (), s32[]{:S(2)}) async-start(), calls=%async_computation.3 | async-start | bytes 3145728 | tf_op jit(solution)/shard_map/reduce_scatter | solution.py:74
  15.7 1.2 copy-start.1
  16.9 8.7 %copy-start.4 = (s32[32]{0:T(128)S(1)}, s32[32]{0:T(128)}, u32[]{:S(2)}) copy-start(s32[32]{0:T(128)} %param.15) | copy-start | bytes 388
  16.9 8.7 %copy-start.5 = (s32[32]{0:T(128)S(1)}, s32[32]{0:T(128)}, u32[]{:S(2)}) copy-start(s32[32]{0:T(128)} %param.14) | copy-start | bytes 388
  16.9 8.9 %copy-start.6 = (s32[128]{0:T(128)S(1)}, s32[128]{0:T(128)}, u32[]{:S(2)}) copy-start(s32[128]{0:T(128)} %param.13) | copy-start | bytes 1540
  16.9 9.0 %copy-start.2 = (bf16[128,512]{1,0:T(8,128)(2,1)S(1)}, bf16[128,512]{1,0:T(8,128)(2,1)}, u32[]{:S(2)}) copy-start(bf16[128,512]{1,0:T(8,128)(2,1)} %param.9) | copy-start | bytes 393220
  18.2 46.0 %all-to-all-start = ((bf16[128,16,256]{0,2,1:T(8,128)(2,1)}), bf16[128,16,256]{0,2,1:T(8,128)(2,1)}, u32[]{:S(2)}, u32[]{:S(2)}) async-start(bf16[128,16,256]{0,2,1:T(8,128)(2,1)} %bitcast.7), calls=%async_computation.1 | async-start | bytes 2097152 | tf_op jit(solution)/shard_map/all_to_all | solution.py:45
  25.6 95.8 %all-gather.2.cloned.1.call-start = ((), (), s32[]{:S(2)}) async-start(), calls=%async_computation.4 | async-start | bytes 4456448 | tf_op jit(solution)/shard_map/all_gather | solution.py:68
  39.1 34.9 %copy-start.3 = (bf16[128,32]{0,1:T(8,128)(2,1)}, bf16[128,32]{0,1:T(8,128)(2,1)S(1)}, u32[]{:S(2)}) copy-start(bf16[128,32]{0,1:T(8,128)(2,1)S(1)} %psum.7) | copy-start | bytes 24580
  70.5 10.4 %all-to-all-start.1 = ((bf16[128,16,32]{0,2,1:T(8,128)(2,1)}), bf16[128,16,32]{0,2,1:T(8,128)(2,1)S(1)}, u32[]{:S(2)}, u32[]{:S(2)}) async-start(bf16[128,16,32]{0,2,1:T(8,128)(2,1)} %bitcast.14), calls=%async_computation.2 | async-start | bytes 262144 | tf_op jit(solution)/shard_map/all_to_all | solution.py:48
  74.0 32.3 %slice-start = ((bf16[128,32]{0,1:T(8,128)(2,1)}), bf16[128,16]{0,1:T(8,128)(2,1)S(1)}, s32[]{:S(2)}) async-start(bf16[128,32]{0,1:T(8,128)(2,1)} %copy-done.3), calls=%async_computation.5 | async-start | bytes 8192 | tf_op jit(solution)/shard_map/slice | solution.py:75
Sparse Core Ops, SparseCore 0:
  15.8 34.1 reduce-scatter.1
Sparse Core Ops, SparseCore 1:
  69.8 51.5 all-gather.1

commit v2 on v1

--- a/solution.py
+++ b/solution.py
@@ -1,6 +1,9 @@
+import functools
 import jax
 import jax.numpy as jnp
 from jax import lax
+from jax.experimental import pallas as pl
+from jax.experimental.pallas import tpu as pltpu
 from jax.sharding import PartitionSpec as P
 
 adapter_scale = 2.0
@@ -82,6 +85,318 @@
     return (input_gradient, down_gradient, up_gradient)
 
 
+MESH = pl.DeviceIdType.MESH
+
+
+def kernel(
+    dp,
+    x_ref, kc_ref, kct_ref, up_ref, slot_ref, down_hbm, w_hbm,
+    gathered_ref, ingrad_ref,
+    down, w, x_all, kct_all, part, part_in, low_all, spread_h, spread_g, send_f, recv_f, own_f,
+    local_sem, x_sem, k_sem, part_sem, low_sem, f_sem, z_sem, y_sem, c_sem,
+):
+    bf16, f32 = jnp.bfloat16, jnp.float32
+    tokens, feats = x_ref.shape
+    pairs = down.shape[0]
+    heads = kc_ref.shape[1]
+    rank = part.shape[0] // 2
+    tenants = pairs // rank
+    cols = feats // dp
+    krows = heads // dp
+    me = lax.axis_index("dp")
+    ten = lax.axis_index("tensor")
+    other = 1 - ten
+    zn = dp // 4
+    z, y, core = me // 4, (me // 2) % 2, me % 2
+
+    def w_half(t, i):
+        rows = pl.ds(pl.multiple_of(t * feats, feats), feats)
+        return pltpu.make_async_copy(w_hbm.at[rows], w.at[i], local_sem.at[i])
+
+    load_down = pltpu.make_async_copy(down_hbm, down, local_sem.at[2])
+    load_down.start()
+    load_other = w_half(other, 0)
+    load_other.start()
+    load_own = w_half(ten, 1)
+    load_own.start()
+
+    barrier = pltpu.get_barrier_semaphore()
+    for o in range(1, dp):
+        pl.semaphore_signal(
+            barrier, inc=1, device_id=(lax.rem(me + o, dp), ten), device_id_type=MESH
+        )
+    pl.semaphore_signal(barrier, inc=1, device_id=(me, other), device_id_type=MESH)
+    pl.semaphore_wait(barrier, dp)
+
+    def remote(src, dst, sems, i, to):
+        return pltpu.make_async_remote_copy(
+            src_ref=src, dst_ref=dst, send_sem=sems.at[0, i], recv_sem=sems.at[1, i],
+            device_id=to, device_id_type=MESH,
+        )
+
+    def span(i, n):
+        return pl.ds(pl.multiple_of(i * n, n), n)
+
+    x_copies, k_copies = [], []
+    for o in range(1, dp):
+        p = lax.rem(me + o, dp)
+        c = remote(x_ref.at[:, span(p, cols)], x_all.at[span(me, tokens)], x_sem, o, (p, ten))
+        c.start()
+        x_copies.append(c)
+        c = remote(
+            kct_ref.at[span(p, krows)], kct_all.at[:, span(me, tokens)], k_sem, o, (p, ten)
+        )
+        c.start()
+        k_copies.append(c)
+    x_all[span(me, tokens), :] = x_ref[:, span(me, cols)]
+    kct_all[:, span(me, tokens)] = kct_ref[span(me, krows), :]
+
+    nt = (((1,), (1,)), ((), ()))
+    slot_row = slot_ref[...].astype(f32)
+    tenant_of_row = lax.broadcasted_iota(jnp.int32, (tenants, rank, tokens), 0).astype(f32)
+
+    def pick(values):
+        v = values.reshape(tenants, rank, tokens)
+        return jnp.sum(jnp.where(tenant_of_row == slot_row[None], v, 0.0), axis=0)
+
+    def spread(values, slots):
+        full = jnp.where(tenant_of_row == slots[None], values[None], 0.0)
+        return full.astype(bf16).reshape(pairs, tokens)
+
+    part[rank:, :] = pick(lax.dot_general(up_ref[...], kc_ref[...], nt, preferred_element_type=f32))
+    load_down.wait()
+    part[:rank, :] = pick(lax.dot_general(down[...], x_ref[...], nt, preferred_element_type=f32))
+    part_copy = remote(part, part_in, part_sem, 0, (me, other))
+    part_copy.start()
+
+    chunk = 512
+    groups = f_sem.shape[1]
+    per_group = feats // chunk // groups
+    load_other.wait()
+    f_copies = []
+    for g in range(groups):
+
+        @pl.loop(g * per_group, (g + 1) * per_group)
+        def _(j):
+            at = span(j, chunk)
+            send_f[:, at] = lax.dot_general(
+                kc_ref[...], w[0, at, :], nt, preferred_element_type=f32
+            ).astype(bf16)
+
+        width = per_group * chunk
+        at = pl.ds(g * width, width)
+        c = remote(send_f.at[:, at], recv_f.at[:, at], f_sem, g, (me, other))
+        c.start()
+        f_copies.append(c)
+
+    part_copy.wait()
+    total = part[...] + part_in[...]
+    low_all[me, : 2 * rank, :] = total.astype(bf16)
+    low_all[me, 2 * rank :, :] = jnp.broadcast_to(slot_row, (rank, tokens)).astype(bf16)
+    low_copies = []
+    for o in range(1, dp):
+        c = remote(low_all.at[me], low_all.at[me], low_sem, o, (lax.rem(me + o, dp), ten))
+        c.start()
+        low_copies.append(c)
+
+    low_g = total[rank:, :].astype(bf16).astype(f32)
+    mine = spread(low_g, jnp.broadcast_to(slot_row, (rank, tokens)))
+    tn = (((0,), (0,)), ((), ()))
+    load_own.wait()
+
+    @pl.loop(0, feats // chunk)
+    def _(j):
+        at = span(j, chunk)
+        own_f[:, at] = lax.dot_general(
+            kc_ref[...], w[1, at, :], nt, preferred_element_type=f32
+        ) + adapter_scale * lax.dot_general(mine, down[:, at], tn, preferred_element_type=f32)
+
+    for c in low_copies:
+        c.wait()
+
+    @pl.loop(0, dp)
+    def _(s):
+        at = span(s, tokens)
+        slots = low_all[s, 2 * rank :, :].astype(f32)
+        spread_h[:, at] = spread(low_all[s, :rank, :].astype(f32), slots)
+        spread_g[:, at] = spread(low_all[s, rank : 2 * rank, :].astype(f32), slots)
+
+    for c in k_copies:
+        c.wait()
+    up_piece = adapter_scale * lax.dot_general(
+        kct_all[...], spread_h[...], nt, preferred_element_type=f32
+    )
+    folds = pairs // cols
+    for i in range(folds):
+        gathered_ref[pairs + i * krows : pairs + (i + 1) * krows, span(me, cols)] = up_piece[
+            :, i * cols : (i + 1) * cols
+        ].astype(bf16)
+    for c in x_copies:
+        c.wait()
+    gathered_ref[:pairs, span(me, cols)] = (
+        adapter_scale * jnp.dot(spread_g[...], x_all[...], preferred_element_type=f32)
+    ).astype(bf16)
+
+    half = gathered_ref.shape[0] // 2
+    pending = []
+
+    def block(src, h):
+        return gathered_ref.at[pl.ds(h * half, half), span(src, cols)]
+
+    def index(zz, yy, cc):
+        return (zz * 2 + yy) * 2 + cc
+
+    def push(src, h, sems, i, to):
+        c = remote(block(src, h), block(src, h), sems, i, (to, ten))
+        c.start()
+        pending.append(c)
+        return c
+
+    right = index(lax.rem(z + 1, zn), y, core)
+    left = index(lax.rem(z + zn - 1, zn), y, core)
+    across = index(z, 1 - y, core)
+    twin = index(z, y, 1 - core)
+
+    def ring(step, h):
+        away = zn - step if h == 0 else step
+        src = index(lax.rem(z + away, zn), y, core)
+        c = None
+        if step < zn - 1:
+            c = push(src, h, z_sem, 2 * step + h, right if h == 0 else left)
+        i = 2 * step + h
+        yc = push(src, h, y_sem, i, across)
+        push(src, h, c_sem, i, twin)
+        return c, yc, away
+
+    now = [ring(0, h) for h in range(2)]
+
+    for c in f_copies:
+        c.wait()
+
+    @pl.loop(0, feats // chunk)
+    def _(j):
+        at = span(j, chunk)
+        ingrad_ref[:, at] = (own_f[:, at] + recv_f[:, at].astype(f32)).astype(bf16)
+
+    for step in range(1, zn + 1):
+        later = []
+        for h in range(2):
+            if step < zn:
+                now[h][0].wait_recv()
+                later.append(ring(step, h))
+        for h in range(2):
+            _, yc, away = now[h]
+            yc.wait_recv()
+            src = index(lax.rem(z + away, zn), 1 - y, core)
+            push(src, h, c_sem, 2 * zn + 2 * (step - 1) + h, twin)
+        now = later
+    for c in pending:
+        c.wait_send()
+    for i in range(4 * zn):
+        remote(block(0, 0), block(0, 0), c_sem, i, (twin, ten)).wait_recv()
+
+
+def per_device_kernel(
+    dp,
+    normed_input,
+    key_cotangent,
+    frozen_key_weight,
+    adapter_down_maps,
+    adapter_up_maps,
+    document_of_token,
+    tenant_of_document,
+    tenant_slot_index,
+):
+    tenant_count, feats, rank = adapter_down_maps.shape
+    heads = adapter_up_maps.shape[2]
+    tokens = normed_input.shape[0]
+    pairs = tenant_count * rank
+    cols = feats // dp
+    krows = heads // dp
+    zn = dp // 4
+    rows = pairs + krows * (pairs // cols)
+    bf16, f32 = jnp.bfloat16, jnp.float32
+    tenants = jnp.arange(tenant_count, dtype=jnp.int32)
+    slot_of_doc = jnp.sum(
+        jnp.where(tenant_of_document[:, None] == tenants[None, :], tenant_slot_index[None, :], 0), axis=1
+    )
+    docs = jnp.arange(tenant_of_document.shape[0], dtype=jnp.int32)
+    slot = jnp.sum(
+        jnp.where(document_of_token[None, :] == docs[:, None], slot_of_doc[:, None], 0),
+        axis=0,
+        keepdims=True,
+    )
+    down_rows = jnp.transpose(adapter_down_maps, (0, 2, 1)).reshape(pairs, feats)
+    up_rows = adapter_up_maps.reshape(pairs, heads)
+    vmem = pl.BlockSpec(memory_space=pltpu.VMEM)
+    hbm = pl.BlockSpec(memory_space=pl.ANY)
+    dma = pltpu.SemaphoreType.DMA
+    gathered, input_gradient = pl.pallas_call(
+        functools.partial(kernel, dp),
+        out_shape=(
+            jax.ShapeDtypeStruct((rows, feats), bf16),
+            jax.ShapeDtypeStruct((tokens, feats), bf16),
+        ),
+        in_specs=[vmem] * 5 + [hbm] * 2,
+        out_specs=(vmem, vmem),
+        scratch_shapes=[
+            pltpu.VMEM((pairs, feats), bf16),
+            pltpu.VMEM((2, feats, heads), bf16),
+            pltpu.VMEM((tokens * dp, cols), bf16),
+            pltpu.VMEM((krows, tokens * dp), bf16),
+            pltpu.VMEM((2 * rank, tokens), f32),
+            pltpu.VMEM((2 * rank, tokens), f32),
+            pltpu.VMEM((dp, 3 * rank, tokens), bf16),
+            pltpu.VMEM((pairs, tokens * dp), bf16),
+            pltpu.VMEM((pairs, tokens * dp), bf16),
+            pltpu.VMEM((tokens, feats), bf16),
+            pltpu.VMEM((tokens, feats), bf16),
+            pltpu.VMEM((tokens, feats), f32),
+            dma((3,)),
+            dma((2, dp)),
+            dma((2, dp)),
+            dma((2, 1)),
+            dma((2, dp)),
+            dma((2, 4)),
+            dma((2, 2 * zn)),
+            dma((2, 2 * zn)),
+            dma((2, 4 * zn)),
+        ],
+        compiler_params=pltpu.CompilerParams(
+            collective_id=0, has_side_effects=True, vmem_limit_bytes=60 * 1024 * 1024
+        ),
+    )(
+        normed_input,
+        key_cotangent,
+        key_cotangent.T,
+        up_rows,
+        slot,
+        down_rows,
+        frozen_key_weight,
+    )
+    down_gradient = jnp.transpose(
+        gathered[:pairs].reshape(tenant_count, rank, feats), (0, 2, 1)
+    )
+    up = gathered[pairs:].reshape(pairs // cols, krows, dp, cols)
+    up_gradient = jnp.transpose(up, (0, 3, 2, 1)).reshape(tenant_count, rank, heads)
+    return (input_gradient, down_gradient, up_gradient)
+
+
+def fits_kernel(dp, tensor, args):
+    tokens, feats = args[0].shape
+    heads = args[1].shape[1]
+    tenant_count, _, rank = args[3].shape
+    pairs = tenant_count * rank
+    if tensor != 2 or dp % 4 or dp < 8 or tokens != 128 or feats % (dp * 128) or heads % (dp * 16):
+        return False
+    cols = feats // dp
+    rows = pairs + (heads // dp) * (pairs // cols)
+    return (
+        feats % 2048 == 0 and pairs % cols == 0 and rank % 16 == 0
+        and rows % 32 == 0 and tenant_count <= 256
+    )
+
+
 def solution(mesh):
     in_specs = (
         P("dp", "tensor"),
@@ -96,6 +411,9 @@
     out_specs = (P("dp", "tensor"), P(None, "tensor", None), P(None, None, "tensor"))
 
     def body(*args):
-        return per_device(mesh.shape["dp"], mesh.shape["tensor"], *args)
+        dp, tensor = mesh.shape["dp"], mesh.shape["tensor"]
+        if fits_kernel(dp, tensor, args):
+            return per_device_kernel(dp, *args)
+        return per_device(dp, tensor, *args)
 
     return jax.shard_map(body, mesh=mesh, in_specs=in_specs, out_specs=out_specs, check_vma=False)

time: 134 us -> 92.7 us (0.69)
  Pallas kernels: 0 us -> 74.7 us
  blocking collectives: 54.6 us -> 0 us
  matrix products: 23.4 us -> 0 us
  waiting for transfers between devices: 15.9 us -> 0 us
  between operations: 15.6 us -> 0.66 us
  starting transfers between devices: 10.9 us -> 0 us
  local copies, waits for them, and re-layouts: 11.3 us -> 14.8 us
    pallas_call x0 -> x1, Pallas kernels: none -> 74.7 us  [per_device_kernel(): pl.pallas_call(functools.partial(kernel, dp), out_shape=(jax.ShapeDtypeSt...]
    all_gather x2 -> x0, blocking collectives: 47 us -> none  [the longest x1 23.6 us: per_device(): up_flat = lax.all_gather(up_piece, 'dp', axis=1, tiled=True)]
    dot_general x6 -> x0, matrix products: 23.4 us -> none  [the longest x1 7.64 us: per_device(): lax.dot_general(key_cotangent, frozen_key_weight, contract_last, preferre...]
    all_to_all x2 -> x0, starting transfers between devices: 10.8 us -> none  [the longest x1 7.34 us: per_device(): lax.all_to_all(normed_input.reshape(tokens, dp_count, -1), 'dp', split_ax...]
    all_gather x1 -> x0, waiting for transfers between devices: 8.96 us -> none  [per_device(): down_flat = lax.all_gather(down_piece, 'dp', axis=1, tiled=True)]
    psum x1 -> x0, blocking collectives: 7.53 us -> none  [per_device(): lax.psum(jnp.concatenate([h_part, g_part], axis=1), 'tensor').astype(bf16)]
    all_to_all x2 -> x0, waiting for transfers between devices: 6.89 us -> none  [the longest x1 6.89 us: per_device(): lax.all_to_all(key_cotangent.reshape(tokens, dp_count, -1), 'dp', split_a...]
    slice x3 -> x2, local copies, waits for them, and re-layouts: 0.02 us -> 5.78 us  [the longest x1 4.7 us: per_device_kernel(): gathered[:pairs].reshape(tenant_count, rank, feats)]
  transfers between devices with their start and end apart: 4 -> 0, of which waited for: 2 -> 0; matrix products, arithmetic and copies ran while one was open for 17% -> 0% of each run, Pallas kernels for 0% -> 0%
where the time goes in v2:
time: 92.7 us; the launch traced here: 92.3 us
  Pallas kernels  74.7 us (81%)
  local copies, waits for them, and re-layouts  14.8 us (16%)
  other arithmetic  2.11 us (2%)
    pallas_call x1, Pallas kernels, per_device_kernel(): pl.pallas_call(functools.partial(kernel, dp), out_shape=(jax.ShapeDtypeSt...  74.7 us
    slice x1, local copies, waits for them, and re-layouts, per_device_kernel(): gathered[:pairs].reshape(tenant_count, rank, feats)  4.7 us
    unnamed x3, local copies, waits for them, and re-layouts  4.05 us
    reshape x1, local copies, waits for them, and re-layouts, per_device_kernel(): jnp.transpose(up, (0, 3, 2, 1)).reshape(tenant_count, rank, heads)  2.75 us
    reshape x1, local copies, waits for them, and re-layouts, per_device_kernel(): up = gathered[pairs:].reshape(pairs // cols, krows, dp, cols)  2.2 us

profile of v2, /device:TPU:1, one launch (start us, length us, event | category | flops | bytes accessed | tf_op | source)
XLA Modules:
  0.0 92.3 jit_solution(4720733350413424040)
XLA Ops:
  0.6 0.9 select_reduce_fusion.1
  1.5 1.3 %select_reduce_fusion = s32[128]{0:T(128)} fusion(s32[32]{0:T(128)S(1)} %select_reduce_fusion.1, s32[128]{0:T(128)} %param.13), kind=kLoop, calls=%fused_computation | loop fusion | flops 12160 | bytes 1152 | tf_op jit(solution)/shard_map/reduce_sum | solution.py:324
  2.7 1.7 %copy.15 = bf16[128,512]{0,1:T(8,128)(2,1)} copy(bf16[128,512]{1,0:T(8,128)(2,1)} %kc_ref.1) | data formatting | bytes 262144 | tf_op args[1]
  4.4 74.7 %shard_map.103 = (bf16[576,4096]{1,0:T(8,128)(2,1)}, bf16[128,4096]{1,0:T(8,128)(2,1)}) custom-call(bf16[128,4096]{1,0:T(8,128)(2,1)} %x_ref.1, bf16[128,512]{1,0:T(8,128)(2,1)} %kc_ref.1, bf16[512,128]{1,0:T(8,128)(2,1)} %bitcast.20, bf16[512,512]{1,0:T(8,128)(2,1)} %bitcast.21, s32[1,128]{1,0:T(1,128)} %bitcast.22, bf16[512,4096]{1,0:T(8,128)(2,1)} %bitcast.17, ...), custom_call_target="tpu_custom_call" | custom-call | tf_op jit(solution)/shard_map/pallas_call | solution.py:334
  79.2 1.1 %slice.7 = bf16[64,4096]{1,0:T(8,128)(2,1)S(1)} slice(bf16[576,4096]{1,0:T(8,128)(2,1)} %get-tuple-element.6), slice={[512:576], [0:4096]} | slice | bytes 1048576 | tf_op jit(solution)/shard_map/slice | solution.py:380
  80.2 4.7 %slice.6 = bf16[512,4096]{1,0:T(8,128)(2,1)} slice(bf16[576,4096]{1,0:T(8,128)(2,1)} %get-tuple-element.6), slice={[0:512], [0:4096]} | slice | bytes 8388608 | tf_op jit(solution)/shard_map/slice | solution.py:378
  84.9 0.1 copy.17
  85.0 2.2 %copy.16 = bf16[2,32,16,256]{1,2,3,0:T(8,128)(2,1)S(1)} copy(bf16[2,32,16,256]{3,2,1,0:T(8,128)(2,1)S(1)} %bitcast.18) | data formatting | bytes 1048576 | tf_op jit(solution)/shard_map/reshape | solution.py:380
  87.2 2.8 %reshape.29 = bf16[32,16,512]{2,1,0:T(8,128)(2,1)} reshape(bf16[2,256,16,32]{3,2,1,0:T(8,128)(2,1)S(1)} %bitcast.15) | data formatting | bytes 1048576 | tf_op jit(solution)/shard_map/reshape | solution.py:381
  90.0 2.3 %copy.19 = bf16[128,4096]{1,0:T(8,128)(2,1)} copy(bf16[128,4096]{1,0:T(8,128)(2,1)} %get-tuple-element.10) | data formatting | bytes 2097152

commit v3 on v2

--- a/solution.py
+++ b/solution.py
@@ -91,9 +91,9 @@
 def kernel(
     dp,
     x_ref, kc_ref, kct_ref, up_ref, slot_ref, down_hbm, w_hbm,
-    gathered_ref, ingrad_ref,
-    down, w, x_all, kct_all, part, part_in, low_all, spread_h, spread_g, send_f, recv_f, own_f,
-    local_sem, x_sem, k_sem, part_sem, low_sem, f_sem, z_sem, y_sem, c_sem,
+    down_out, up_out, ingrad_ref,
+    gathered_ref, down, w, x_all, kct_all, part, part_in, low_all, spread_h, spread_g, send_f, recv_f, own_f,
+    local_sem, x_sem, k_sem, part_sem, low_sem, f_sem, z_sem, y_sem, c_sem, out_sem,
 ):
     bf16, f32 = jnp.bfloat16, jnp.float32
     tokens, feats = x_ref.shape
@@ -137,17 +137,31 @@
     def span(i, n):
         return pl.ds(pl.multiple_of(i * n, n), n)
 
-    x_copies, k_copies = [], []
+    half = cols // 2
+
+    def half_of(src, h):
+        return pl.ds(pl.multiple_of(src * cols + h * half, half), half)
+
+    x_copies, k_copies = [[], []], []
     for o in range(1, dp):
         p = lax.rem(me + o, dp)
-        c = remote(x_ref.at[:, span(p, cols)], x_all.at[span(me, tokens)], x_sem, o, (p, ten))
-        c.start()
-        x_copies.append(c)
         c = remote(
             kct_ref.at[span(p, krows)], kct_all.at[:, span(me, tokens)], k_sem, o, (p, ten)
         )
         c.start()
         k_copies.append(c)
+    for h in range(2):
+        for o in range(1, dp):
+            p = lax.rem(me + o, dp)
+            c = remote(
+                x_ref.at[:, half_of(p, h)],
+                x_all.at[span(me, tokens), pl.ds(h * half, half)],
+                x_sem,
+                h * dp + o,
+                (p, ten),
+            )
+            c.start()
+            x_copies[h].append(c)
     x_all[span(me, tokens), :] = x_ref[:, span(me, cols)]
     kct_all[:, span(me, tokens)] = kct_ref[span(me, krows), :]
 
@@ -231,17 +245,21 @@
         gathered_ref[pairs + i * krows : pairs + (i + 1) * krows, span(me, cols)] = up_piece[
             :, i * cols : (i + 1) * cols
         ].astype(bf16)
-    for c in x_copies:
-        c.wait()
-    gathered_ref[:pairs, span(me, cols)] = (
-        adapter_scale * jnp.dot(spread_g[...], x_all[...], preferred_element_type=f32)
-    ).astype(bf16)
-
-    half = gathered_ref.shape[0] // 2
-    pending = []
+
+    def finish_half(h):
+        for c in x_copies[h]:
+            c.wait()
+        gathered_ref[:pairs, half_of(me, h)] = (
+            adapter_scale
+            * jnp.dot(
+                spread_g[...], x_all[:, h * half : (h + 1) * half], preferred_element_type=f32
+            )
+        ).astype(bf16)
+
+    pending, outs = [], []
 
     def block(src, h):
-        return gathered_ref.at[pl.ds(h * half, half), span(src, cols)]
+        return gathered_ref.at[:, half_of(src, h)]
 
     def index(zz, yy, cc):
         return (zz * 2 + yy) * 2 + cc
@@ -252,23 +270,47 @@
         pending.append(c)
         return c
 
+    def put(src, h):
+        c = pltpu.make_async_copy(
+            gathered_ref.at[pl.ds(0, pairs), half_of(src, h)],
+            down_out.at[:, half_of(src, h)],
+            out_sem.at[len(outs)],
+        )
+        c.start()
+        outs.append(c)
+
     right = index(lax.rem(z + 1, zn), y, core)
     left = index(lax.rem(z + zn - 1, zn), y, core)
     across = index(z, 1 - y, core)
     twin = index(z, y, 1 - core)
+    z_copies, y_copies = {}, {}
+
+    def layer(step, h):
+        return lax.rem(z + (zn - step if h == 0 else step), zn)
 
     def ring(step, h):
-        away = zn - step if h == 0 else step
-        src = index(lax.rem(z + away, zn), y, core)
-        c = None
+        src = index(layer(step, h), y, core)
+        if step > 0:
+            z_copies[step - 1, h].wait_recv()
+        i = 2 * step + h
         if step < zn - 1:
-            c = push(src, h, z_sem, 2 * step + h, right if h == 0 else left)
-        i = 2 * step + h
-        yc = push(src, h, y_sem, i, across)
+            z_copies[step, h] = push(src, h, z_sem, i, right if h == 0 else left)
+        y_copies[step, h] = push(src, h, y_sem, i, across)
         push(src, h, c_sem, i, twin)
-        return c, yc, away
-
-    now = [ring(0, h) for h in range(2)]
+        put(src, h)
+
+    def pass_on(step, h):
+        y_copies[step, h].wait_recv()
+        src = index(layer(step, h), 1 - y, core)
+        push(src, h, c_sem, 2 * zn + 2 * step + h, twin)
+        put(src, h)
+
+    finish_half(0)
+    ring(0, 0)
+    ring(1, 0)
+    pass_on(0, 0)
+    finish_half(1)
+    ring(0, 1)
 
     for c in f_copies:
         c.wait()
@@ -278,22 +320,27 @@
         at = span(j, chunk)
         ingrad_ref[:, at] = (own_f[:, at] + recv_f[:, at].astype(f32)).astype(bf16)
 
-    for step in range(1, zn + 1):
-        later = []
-        for h in range(2):
-            if step < zn:
-                now[h][0].wait_recv()
-                later.append(ring(step, h))
-        for h in range(2):
-            _, yc, away = now[h]
-            yc.wait_recv()
-            src = index(lax.rem(z + away, zn), 1 - y, core)
-            push(src, h, c_sem, 2 * zn + 2 * (step - 1) + h, twin)
-        now = later
+    for step in range(2, zn + 1):
+        if step < zn:
+            ring(step, 0)
+        pass_on(step - 1, 0)
+        ring(step - 1, 1)
+        pass_on(step - 2, 1)
+    pass_on(zn - 1, 1)
+    for yy in range(2):
+        for step in range(zn):
+            for h in range(2):
+                i = 2 * zn * yy + 2 * step + h
+                remote(block(0, 0), block(0, 0), c_sem, i, (twin, ten)).wait_recv()
+                put(index(layer(step, h), y if yy == 0 else 1 - y, 1 - core), h)
+    for i in range(folds):
+        rows = gathered_ref[pairs + i * krows : pairs + (i + 1) * krows, :].astype(f32)
+        stacked = jnp.concatenate([rows[:, p * cols : (p + 1) * cols] for p in range(dp)], axis=0)
+        up_out[i * cols : (i + 1) * cols, :] = stacked.T.astype(bf16)
     for c in pending:
         c.wait_send()
-    for i in range(4 * zn):
-        remote(block(0, 0), block(0, 0), c_sem, i, (twin, ten)).wait_recv()
+    for c in outs:
+        c.wait()
 
 
 def per_device_kernel(
@@ -331,15 +378,17 @@
     vmem = pl.BlockSpec(memory_space=pltpu.VMEM)
     hbm = pl.BlockSpec(memory_space=pl.ANY)
     dma = pltpu.SemaphoreType.DMA
-    gathered, input_gradient = pl.pallas_call(
+    down_flat, up_flat, input_gradient = pl.pallas_call(
         functools.partial(kernel, dp),
         out_shape=(
-            jax.ShapeDtypeStruct((rows, feats), bf16),
+            jax.ShapeDtypeStruct((pairs, feats), bf16),
+            jax.ShapeDtypeStruct((pairs, heads), bf16),
             jax.ShapeDtypeStruct((tokens, feats), bf16),
         ),
         in_specs=[vmem] * 5 + [hbm] * 2,
-        out_specs=(vmem, vmem),
+        out_specs=(hbm, vmem, vmem),
         scratch_shapes=[
+            pltpu.VMEM((rows, feats), bf16),
             pltpu.VMEM((pairs, feats), bf16),
             pltpu.VMEM((2, feats, heads), bf16),
             pltpu.VMEM((tokens * dp, cols), bf16),
@@ -353,7 +402,7 @@
             pltpu.VMEM((tokens, feats), bf16),
             pltpu.VMEM((tokens, feats), f32),
             dma((3,)),
-            dma((2, dp)),
+            dma((2, 2 * dp)),
             dma((2, dp)),
             dma((2, 1)),
             dma((2, dp)),
@@ -361,6 +410,7 @@
             dma((2, 2 * zn)),
             dma((2, 2 * zn)),
             dma((2, 4 * zn)),
+            dma((2 * dp,)),
         ],
         compiler_params=pltpu.CompilerParams(
             collective_id=0, has_side_effects=True, vmem_limit_bytes=60 * 1024 * 1024
@@ -375,10 +425,9 @@
         frozen_key_weight,
     )
     down_gradient = jnp.transpose(
-        gathered[:pairs].reshape(tenant_count, rank, feats), (0, 2, 1)
-    )
-    up = gathered[pairs:].reshape(pairs // cols, krows, dp, cols)
-    up_gradient = jnp.transpose(up, (0, 3, 2, 1)).reshape(tenant_count, rank, heads)
+        down_flat.reshape(tenant_count, rank, feats), (0, 2, 1)
+    )
+    up_gradient = up_flat.reshape(tenant_count, rank, heads)
     return (input_gradient, down_gradient, up_gradient)
 
 
@@ -387,7 +436,7 @@
     heads = args[1].shape[1]
     tenant_count, _, rank = args[3].shape
     pairs = tenant_count * rank
-    if tensor != 2 or dp % 4 or dp < 8 or tokens != 128 or feats % (dp * 128) or heads % (dp * 16):
+    if tensor != 2 or dp % 4 or dp < 8 or tokens != 128 or feats % (dp * 256) or heads % (dp * 16):
         return False
     cols = feats // dp
     rows = pairs + (heads // dp) * (pairs // cols)

time: 92.7 us -> 89.5 us (0.965)
  local copies, waits for them, and re-layouts: 14.8 us -> 9.5 us
  Pallas kernels: 74.7 us -> 77 us
    slice x2 -> x0, local copies, waits for them, and re-layouts: 5.78 us -> none  [the longest x1 4.7 us: per_device_kernel(): gathered[:pairs].reshape(tenant_count, rank, feats)]
    unnamed x3 -> x6, local copies, waits for them, and re-layouts: 4.05 us -> 9.5 us
    reshape x2 -> x0, local copies, waits for them, and re-layouts: 4.95 us -> none  [the longest x1 2.75 us: per_device_kernel(): jnp.transpose(up, (0, 3, 2, 1)).reshape(tenant_count, rank, heads)]
    pallas_call x1, Pallas kernels: 74.7 us -> 77 us  [per_device_kernel(): pl.pallas_call(functools.partial(kernel, dp), out_shape=(jax.ShapeDtypeSt...]
where the time goes in v3:
time: 89.5 us; the launch traced here: 89.2 us
  Pallas kernels  77 us (86%)
  local copies, waits for them, and re-layouts  9.5 us (11%)
  other arithmetic  2.11 us (2%)
    pallas_call x1, Pallas kernels, per_device_kernel(): pl.pallas_call(functools.partial(kernel, dp), out_shape=(jax.ShapeDtypeSt...  77 us
    unnamed x6, local copies, waits for them, and re-layouts  9.5 us

profile of v3, /device:TPU:1, one launch (start us, length us, event | category | flops | bytes accessed | tf_op | source)
XLA Modules:
  0.0 89.2 jit_solution(12258582461342710779)
XLA Ops:
  0.6 0.9 select_reduce_fusion.1
  1.5 1.3 %select_reduce_fusion = s32[128]{0:T(128)} fusion(s32[32]{0:T(128)S(1)} %select_reduce_fusion.1, s32[128]{0:T(128)} %param.13), kind=kLoop, calls=%fused_computation | loop fusion | flops 12160 | bytes 1152 | tf_op jit(solution)/shard_map/reduce_sum | solution.py:371
  2.7 1.7 %copy.12 = bf16[128,512]{0,1:T(8,128)(2,1)} copy(bf16[128,512]{1,0:T(8,128)(2,1)} %kc_ref.1) | data formatting | bytes 262144 | tf_op args[1]
  4.4 77.0 %shard_map.103 = (bf16[512,4096]{1,0:T(8,128)(2,1)}, bf16[512,512]{1,0:T(8,128)(2,1)}, bf16[128,4096]{1,0:T(8,128)(2,1)}) custom-call(bf16[128,4096]{1,0:T(8,128)(2,1)} %x_ref.1, bf16[128,512]{1,0:T(8,128)(2,1)} %kc_ref.1, bf16[512,128]{1,0:T(8,128)(2,1)} %bitcast.12, bf16[512,512]{1,0:T(8,128)(2,1)} %bitcast.13, s32[1,128]{1,0:T(1,128)} %bitcast.15, ...), custom_call_target="tpu_custom_call" | custom-call | tf_op jit(solution)/shard_map/pallas_call | solution.py:381
  81.4 2.3 %copy.16 = bf16[128,4096]{1,0:T(8,128)(2,1)} copy(bf16[128,4096]{1,0:T(8,128)(2,1)} %get-tuple-element.12) | data formatting | bytes 2097152
  83.7 0.0 copy-start
  83.7 4.8 %copy.17 = bf16[32,4096,16]{1,2,0:T(8,128)(2,1)} copy(bf16[32,4096,16]{1,2,0:T(8,128)(2,1)} %bitcast.10) | data formatting | bytes 8388608
  88.4 0.0 copy-done
  88.4 0.8 copy.18
Async XLA Ops:
  83.7 4.8 %copy-start = (bf16[512,512]{1,0:T(8,128)(2,1)S(1)}, bf16[512,512]{1,0:T(8,128)(2,1)}, u32[]{:S(2)}) copy-start(bf16[512,512]{1,0:T(8,128)(2,1)} %get-tuple-element.8) | copy-start | bytes 1572868

commit v4 on v3

--- a/solution.py
+++ b/solution.py
@@ -90,9 +90,9 @@
 
 def kernel(
     dp,
-    x_ref, kc_ref, kct_ref, up_ref, slot_ref, down_hbm, w_hbm,
+    x_ref, kc_ref, up_ref, doc_ref, tenant_ref, index_ref, down_hbm, w_hbm,
     down_out, up_out, ingrad_ref,
-    gathered_ref, down, w, x_all, kct_all, part, part_in, low_all, spread_h, spread_g, send_f, recv_f, own_f,
+    kct_ref, gathered_ref, down, w, x_all, kct_all, part, part_in, low_all, spread_h, spread_g, send_f, recv_f, own_f,
     local_sem, x_sem, k_sem, part_sem, low_sem, f_sem, z_sem, y_sem, c_sem, out_sem,
 ):
     bf16, f32 = jnp.bfloat16, jnp.float32
@@ -120,6 +120,7 @@
     load_own = w_half(ten, 1)
     load_own.start()
 
+    kct_ref[...] = kc_ref[...].astype(f32).T.astype(bf16)
     barrier = pltpu.get_barrier_semaphore()
     for o in range(1, dp):
         pl.semaphore_signal(
@@ -155,18 +156,22 @@
             p = lax.rem(me + o, dp)
             c = remote(
                 x_ref.at[:, half_of(p, h)],
-                x_all.at[span(me, tokens), pl.ds(h * half, half)],
+                x_all.at[h, span(me, tokens)],
                 x_sem,
                 h * dp + o,
                 (p, ten),
             )
             c.start()
             x_copies[h].append(c)
-    x_all[span(me, tokens), :] = x_ref[:, span(me, cols)]
+    for h in range(2):
+        x_all[h, span(me, tokens), :] = x_ref[:, half_of(me, h)]
     kct_all[:, span(me, tokens)] = kct_ref[span(me, krows), :]
 
     nt = (((1,), (1,)), ((), ()))
-    slot_row = slot_ref[...].astype(f32)
+    slots_now = jnp.zeros((1, tokens), jnp.int32)
+    for d in range(tenant_ref.shape[0]):
+        slots_now = jnp.where(doc_ref[...] == d, index_ref[tenant_ref[d]], slots_now)
+    slot_row = slots_now.astype(f32)
     tenant_of_row = lax.broadcasted_iota(jnp.int32, (tenants, rank, tokens), 0).astype(f32)
 
     def pick(values):
@@ -242,24 +247,25 @@
     )
     folds = pairs // cols
     for i in range(folds):
-        gathered_ref[pairs + i * krows : pairs + (i + 1) * krows, span(me, cols)] = up_piece[
-            :, i * cols : (i + 1) * cols
-        ].astype(bf16)
+        for h in range(2):
+            gathered_ref[me, h, pairs + i * krows : pairs + (i + 1) * krows, :] = up_piece[
+                :, i * cols + h * half : i * cols + (h + 1) * half
+            ].astype(bf16)
 
     def finish_half(h):
         for c in x_copies[h]:
             c.wait()
-        gathered_ref[:pairs, half_of(me, h)] = (
+        gathered_ref[me, h, :pairs, :] = (
             adapter_scale
             * jnp.dot(
-                spread_g[...], x_all[:, h * half : (h + 1) * half], preferred_element_type=f32
+                spread_g[...], x_all[h], preferred_element_type=f32
             )
         ).astype(bf16)
 
     pending, outs = [], []
 
     def block(src, h):
-        return gathered_ref.at[:, half_of(src, h)]
+        return gathered_ref.at[src, h]
 
     def index(zz, yy, cc):
         return (zz * 2 + yy) * 2 + cc
@@ -272,7 +278,7 @@
 
     def put(src, h):
         c = pltpu.make_async_copy(
-            gathered_ref.at[pl.ds(0, pairs), half_of(src, h)],
+            gathered_ref.at[src, h, pl.ds(0, pairs)],
             down_out.at[:, half_of(src, h)],
             out_sem.at[len(outs)],
         )
@@ -334,8 +340,16 @@
                 remote(block(0, 0), block(0, 0), c_sem, i, (twin, ten)).wait_recv()
                 put(index(layer(step, h), y if yy == 0 else 1 - y, 1 - core), h)
     for i in range(folds):
-        rows = gathered_ref[pairs + i * krows : pairs + (i + 1) * krows, :].astype(f32)
-        stacked = jnp.concatenate([rows[:, p * cols : (p + 1) * cols] for p in range(dp)], axis=0)
+        at = slice(pairs + i * krows, pairs + (i + 1) * krows)
+        stacked = jnp.concatenate(
+            [
+                jnp.concatenate(
+                    [gathered_ref[p, h, at, :].astype(f32) for p in range(dp)], axis=0
+                )
+                for h in range(2)
+            ],
+            axis=1,
+        )
         up_out[i * cols : (i + 1) * cols, :] = stacked.T.astype(bf16)
     for c in pending:
         c.wait_send()
@@ -363,20 +377,12 @@
     zn = dp // 4
     rows = pairs + krows * (pairs // cols)
     bf16, f32 = jnp.bfloat16, jnp.float32
-    tenants = jnp.arange(tenant_count, dtype=jnp.int32)
-    slot_of_doc = jnp.sum(
-        jnp.where(tenant_of_document[:, None] == tenants[None, :], tenant_slot_index[None, :], 0), axis=1
-    )
-    docs = jnp.arange(tenant_of_document.shape[0], dtype=jnp.int32)
-    slot = jnp.sum(
-        jnp.where(document_of_token[None, :] == docs[:, None], slot_of_doc[:, None], 0),
-        axis=0,
-        keepdims=True,
-    )
     down_rows = jnp.transpose(adapter_down_maps, (0, 2, 1)).reshape(pairs, feats)
     up_rows = adapter_up_maps.reshape(pairs, heads)
     vmem = pl.BlockSpec(memory_space=pltpu.VMEM)
-    hbm = pl.BlockSpec(memory_space=pl.ANY)
+    smem = pl.BlockSpec(memory_space=pltpu.SMEM)
+    hbm = pl.BlockSpec(memory_space=pltpu.HBM)
+    anywhere = pl.BlockSpec(memory_space=pl.ANY)
     dma = pltpu.SemaphoreType.DMA
     down_flat, up_flat, input_gradient = pl.pallas_call(
         functools.partial(kernel, dp),
@@ -385,13 +391,14 @@
             jax.ShapeDtypeStruct((pairs, heads), bf16),
             jax.ShapeDtypeStruct((tokens, feats), bf16),
         ),
-        in_specs=[vmem] * 5 + [hbm] * 2,
-        out_specs=(hbm, vmem, vmem),
+        in_specs=[vmem] * 4 + [smem] * 2 + [hbm] * 2,
+        out_specs=(anywhere, vmem, vmem),
         scratch_shapes=[
-            pltpu.VMEM((rows, feats), bf16),
+            pltpu.VMEM((heads, tokens), bf16),
+            pltpu.VMEM((dp, 2, rows, cols // 2), bf16),
             pltpu.VMEM((pairs, feats), bf16),
             pltpu.VMEM((2, feats, heads), bf16),
-            pltpu.VMEM((tokens * dp, cols), bf16),
+            pltpu.VMEM((2, tokens * dp, cols // 2), bf16),
             pltpu.VMEM((krows, tokens * dp), bf16),
             pltpu.VMEM((2 * rank, tokens), f32),
             pltpu.VMEM((2 * rank, tokens), f32),
@@ -413,14 +420,15 @@
             dma((2 * dp,)),
         ],
         compiler_params=pltpu.CompilerParams(
-            collective_id=0, has_side_effects=True, vmem_limit_bytes=60 * 1024 * 1024
+            collective_id=0, has_side_effects=True, vmem_limit_bytes=40 * 1024 * 1024
         ),
     )(
         normed_input,
         key_cotangent,
-        key_cotangent.T,
         up_rows,
-        slot,
+        document_of_token.reshape(1, tokens),
+        tenant_of_document,
+        tenant_slot_index,
         down_rows,
         frozen_key_weight,
     )

time: 89.5 us -> 87.1 us (0.973)
  other arithmetic: 2.11 us -> 0 us
  Pallas kernels: 77 us -> 75 us
  local copies, waits for them, and re-layouts: 9.5 us -> 11.1 us
    reduce_sum x2 -> x0, other arithmetic: 2.11 us -> none  [the longest x1 1.26 us: per_device_kernel(): jnp.sum(jnp.where(document_of_token[None, :] == docs[:, None], slot_of_do...]
    pallas_call x1, Pallas kernels: 77 us -> 75 us  [per_device_kernel(): pl.pallas_call(functools.partial(kernel, dp), out_shape=(jax.ShapeDtypeSt...]
    unnamed x6 -> x17, local copies, waits for them, and re-layouts: 9.5 us -> 11.1 us
where the time goes in v4:
time: 87.1 us; the launch traced here: 86.8 us
  Pallas kernels  75 us (86%)
  local copies, waits for them, and re-layouts  11.1 us (13%)
    pallas_call x1, Pallas kernels, per_device_kernel(): pl.pallas_call(functools.partial(kernel, dp), out_shape=(jax.ShapeDtypeSt...  75 us
    unnamed x17, local copies, waits for them, and re-layouts  11.1 us

profile of v4, /device:TPU:1, one launch (start us, length us, event | category | flops | bytes accessed | tf_op | source)
XLA Modules:
  0.0 86.8 jit_solution(9443097453780336546)
XLA Ops:
  0.6 0.0 copy-start
  0.6 2.2 %copy-done = bf16[32,4096,16]{1,2,0:T(8,128)(2,1)S(1)} copy-done((bf16[32,4096,16]{1,2,0:T(8,128)(2,1)S(1)}, bf16[32,4096,16]{1,2,0:T(8,128)(2,1)}, u32[]{:S(2)}) %copy-start) | copy-done | bytes 4194328
  2.8 0.0 copy-start.1
  2.8 1.2 %copy-done.1 = bf16[128,4096]{1,0:T(8,128)(2,1)S(1)} copy-done((bf16[128,4096]{1,0:T(8,128)(2,1)S(1)}, bf16[128,4096]{1,0:T(8,128)(2,1)}, u32[]{:S(2)}) %copy-start.1) | copy-done | bytes 1048600
  4.0 0.0 copy-start.2
  4.0 1.0 %copy-done.2 = bf16[32,16,512]{2,1,0:T(8,128)(2,1)S(1)} copy-done((bf16[32,16,512]{2,1,0:T(8,128)(2,1)S(1)}, bf16[32,16,512]{2,1,0:T(8,128)(2,1)}, u32[]{:S(2)}) %copy-start.2) | copy-done | bytes 524312
  5.1 0.0 copy-start.3
  5.1 0.9 %copy-done.3 = bf16[128,512]{1,0:T(8,128)(2,1)S(1)} copy-done((bf16[128,512]{1,0:T(8,128)(2,1)S(1)}, bf16[128,512]{1,0:T(8,128)(2,1)}, u32[]{:S(2)}) %copy-start.3) | copy-done | bytes 131096
  6.0 0.0 copy-start.4
  6.0 0.7 copy-done.4
  6.7 0.0 copy-start.5
  6.7 0.7 copy-done.5
  7.3 0.0 copy-start.6
  7.3 0.7 copy-done.6
  8.0 75.0 %shard_map.103 = (bf16[512,4096]{1,0:T(8,128)(2,1)S(1)}, bf16[512,512]{1,0:T(8,128)(2,1)S(1)}, bf16[128,4096]{1,0:T(8,128)(2,1)S(1)}) custom-call(bf16[128,4096]{1,0:T(8,128)(2,1)S(1)} %copy-done.1, bf16[128,512]{1,0:T(8,128)(2,1)S(1)} %copy-done.3, bf16[512,512]{1,0:T(8,128)(2,1)S(1)} %bitcast.11, s32[1,128]{1,0:T(1,128)S(1)} %bitcast.13, s32[32]{0:T(128)S(1)} %copy-done.5, ...), custom_call_target="tpu_custom_call" | custom-call | tf_op jit(solution)/shard_map/pallas_call | solution.py:387
  83.0 1.0 %copy.14 = bf16[128,4096]{1,0:T(8,128)(2,1)} copy(bf16[128,4096]{1,0:T(8,128)(2,1)S(1)} %get-tuple-element.12) | data formatting | bytes 2097152
  84.0 2.0 %copy.15 = bf16[32,4096,16]{1,2,0:T(8,128)(2,1)} copy(bf16[32,4096,16]{1,2,0:T(8,128)(2,1)S(1)} %bitcast.10) | data formatting | bytes 8388608
  86.0 0.8 copy.16
Async XLA Ops:
  0.6 2.2 %copy-start = (bf16[32,4096,16]{1,2,0:T(8,128)(2,1)S(1)}, bf16[32,4096,16]{1,2,0:T(8,128)(2,1)}, u32[]{:S(2)}) copy-start(bf16[32,4096,16]{1,2,0:T(8,128)(2,1)} %param.11) | copy-start | bytes 12582916
  2.8 1.2 %copy-start.1 = (bf16[128,4096]{1,0:T(8,128)(2,1)S(1)}, bf16[128,4096]{1,0:T(8,128)(2,1)}, u32[]{:S(2)}) copy-start(bf16[128,4096]{1,0:T(8,128)(2,1)} %x_ref.1) | copy-start | bytes 3145732
  4.0 1.0 %copy-start.2 = (bf16[32,16,512]{2,1,0:T(8,128)(2,1)S(1)}, bf16[32,16,512]{2,1,0:T(8,128)(2,1)}, u32[]{:S(2)}) copy-start(bf16[32,16,512]{2,1,0:T(8,128)(2,1)} %param.12) | copy-start | bytes 1572868
  5.1 0.9 %copy-start.3 = (bf16[128,512]{1,0:T(8,128)(2,1)S(1)}, bf16[128,512]{1,0:T(8,128)(2,1)}, u32[]{:S(2)}) copy-start(bf16[128,512]{1,0:T(8,128)(2,1)} %kc_ref.1) | copy-start | bytes 393220
  6.0 0.7 copy-start.4
  6.7 0.7 copy-start.5
  7.3 0.7 copy-start.6
